TPU v7x, 32 devices: a whole 2x2x4 slice. The times are simulated.
32 devices in a mesh: pano: 2 (over y), seq: 4 (over z), win: 4 (over x, core).
Axes of the slice: x: 2, y: 2, z: 4, core: 2. Of those that a mesh axis runs over, the one named last changes fastest.
Arguments:
- query: bfloat16 [8, 768, 1536], P(('pano', 'win'), 'seq'), parts along dimension 0, may hold values from -8 to 8
- key_image: bfloat16 [8, 768, 1536], P(('pano', 'win'), 'seq'), parts along dimension 0, may hold values from -8 to 8
- value_image: bfloat16 [8, 768, 1536], P(('pano', 'win'), 'seq'), parts along dimension 0, may hold values from -6 to 6
- key_text: bfloat16 [8, 64, 1536], P(('pano', 'win'), 'seq'), parts along dimension 0, may hold values from -6 to 6
- value_text: bfloat16 [8, 64, 1536], P(('pano', 'win'), 'seq'), parts along dimension 0, may hold values from -6 to 6
- prompt_ids: int32 [8, 64], P(('pano', 'win')), parts along dimension 0, may hold values from 0 to 32127, as said below
- blend: int32 [8, 768], P(('pano', 'win'), 'seq'), parts along dimension 0, may hold values from 1 to 15, as said below
- w_out: bfloat16 [1536, 3072], replicated, may hold values from -0.15625 to 0.15625
Outputs:
- joined: bfloat16 [8, 768, 3072], P(('pano', 'win'), 'seq'), parts along dimension 0
There are 2 independent parts, one for each index of `pano`. A program takes and returns all parts, laid end to end along the dimension named above; an argument that names none is the same for every part. Nothing has to cross between parts.
Inputs may be any that keep to these rules, and one draw needn't show every extreme that they name: `prompt_ids`: in each window the nonzero ids form a leading run of 16 or more positions and the rest are 0. At row r and column c < 32, blend[w] plus blend[w - 1] at row r, column c + 32 equals 16, window numbers taken modulo 4.
All inputs are finite; a program needn't handle non-finite values.
Results may differ from a plain program's by a relative error of at most 0.0085.
Values may be sent and summed in bfloat16 or wider, within the bound.
A program may use at most 64 MiB of HBM per device.

v0:
```python
import jax
import jax.numpy as jnp
from jax import lax
from jax.sharding import PartitionSpec as P

HEADS = 12
HEAD_DIM = 128
WCOLS = 64
ROWS_DEV = 3
STRIDE = 32


blend_total = 16.0


def swapped(block, axis, stride):
    count = lax.axis_size(axis)
    route = []
    for low in range(count):
        high = low | 1 << stride
        if high != low and high < count:
            route += [(low, high), (high, low)]
    return lax.ppermute(block, axis, route)


def shifted(block, axis, distance):
    devices = range(lax.axis_size(axis))
    route = [((i - distance) % len(devices), i) for i in devices]
    return lax.ppermute(block, axis, route)


def regroup(stacked, bit_count):
    row_count = stacked.shape[0]
    carried = stacked.reshape(row_count, 1 << bit_count, -1)
    position = lax.axis_index("seq")
    for bit_index in range(bit_count):
        own_bit = position >> bit_index & 1
        paired = carried.reshape(carried.shape[0], carried.shape[1] // 2, 2, carried.shape[2])
        kept_half = lax.dynamic_index_in_dim(paired, own_bit, 2, keepdims=False)
        sent_half = lax.dynamic_index_in_dim(paired, 1 - own_bit, 2, keepdims=False)
        received = swapped(sent_half, "seq", bit_index)
        lower_half = jnp.where(own_bit == 0, kept_half, received)
        upper_half = jnp.where(own_bit == 0, received, kept_half)
        carried = jnp.concatenate([lower_half, upper_half], axis=0)
    return carried.reshape(carried.shape[0], -1)


def ungroup(attended, bit_count):
    carried = attended.reshape(attended.shape[0], 1, attended.shape[1])
    position = lax.axis_index("seq")
    for bit_index in reversed(range(bit_count)):
        own_bit = position >> bit_index & 1
        halves = carried.reshape(2, carried.shape[0] // 2, carried.shape[1], carried.shape[2])
        kept_half = lax.dynamic_index_in_dim(halves, own_bit, 0, keepdims=False)
        sent_half = lax.dynamic_index_in_dim(halves, 1 - own_bit, 0, keepdims=False)
        received = swapped(sent_half, "seq", bit_index)
        lower_half = jnp.where(own_bit == 0, kept_half, received)
        upper_half = jnp.where(own_bit == 0, received, kept_half)
        stacked = jnp.stack([lower_half, upper_half], axis=2)
        carried = stacked.reshape(kept_half.shape[0], -1, kept_half.shape[2])
    return carried.reshape(carried.shape[0], -1)


def absorb(carried, key_value, valid_keys, queries, head_count):
    running, denominator, numerator = carried
    keys_block = key_value[0].reshape(key_value.shape[1], head_count, HEAD_DIM)
    values_block = key_value[1].reshape(key_value.shape[1], head_count, HEAD_DIM)
    scores = jnp.einsum(
        "qhd,khd->qhk", queries, keys_block, preferred_element_type=jnp.float32
    ) * HEAD_DIM ** (-0.5)
    scores = jnp.where(valid_keys[None, None, :], scores, -jnp.inf)
    updated = jnp.maximum(running, jnp.max(scores, axis=2))
    rescale = jnp.exp(running - updated)
    weights = jnp.exp(scores - updated[:, :, None])
    denominator = denominator * rescale + jnp.sum(weights, axis=2)
    product = jnp.einsum(
        "qhk,khd->qhd",
        weights.astype(jnp.bfloat16),
        values_block,
        preferred_element_type=jnp.float32,
    )
    numerator = numerator * rescale[:, :, None] + product
    return (updated, denominator, numerator)


def pass_strips(window_rows):
    from_prev = shifted(window_rows[:, STRIDE:], "win", 1)
    from_next = shifted(window_rows[:, :STRIDE], "win", -1)
    return (from_prev, from_next)


def project_rows(features, w_out):
    flat_rows = features.reshape(-1, features.shape[-1])
    result = jnp.dot(flat_rows, w_out, preferred_element_type=jnp.float32).astype(jnp.bfloat16)
    return result.reshape(ROWS_DEV, -1, w_out.shape[1])


def on_device(query, key_image, value_image, key_text, value_text, prompt_ids, blend, w_out):
    bit_count = 2
    group_size = 1 << bit_count
    image_rows = query.shape[1]
    text_rows = key_text.shape[1]
    key_rows = image_rows + text_rows
    head_count = HEADS // group_size
    stacked = jnp.concatenate(
        [query[0], key_image[0], key_text[0], value_image[0], value_text[0]], axis=0
    )
    grouped = regroup(stacked, bit_count).reshape(group_size, image_rows + 2 * key_rows, -1)
    queries = grouped[:, :image_rows].reshape(group_size * image_rows, head_count, HEAD_DIM)
    keys_grouped = grouped[:, image_rows : image_rows + key_rows].reshape(group_size * key_rows, -1)
    values_grouped = grouped[:, image_rows + key_rows :].reshape(group_size * key_rows, -1)
    key_value = jnp.stack([keys_grouped, values_grouped])
    seq_count = lax.axis_size("seq")
    text_valid = prompt_ids[0].reshape(seq_count, text_rows) != 0
    key_valid = jnp.concatenate([jnp.ones((seq_count, image_rows), jnp.bool_), text_valid], axis=1)
    group_count = seq_count // group_size
    own_group = lax.axis_index("seq") // group_size

    def valid_for(source):
        return lax.dynamic_slice_in_dim(key_valid, source * group_size, group_size, 0).reshape(-1)

    query_count = group_size * image_rows
    initial = (
        jnp.full((query_count, head_count), -jnp.inf, jnp.float32),
        jnp.zeros((query_count, head_count), jnp.float32),
        jnp.zeros((query_count, head_count, HEAD_DIM), jnp.float32),
    )
    carried = absorb(initial, key_value, valid_for(own_group), queries, head_count)

    def one_turn(turn_index, loop_state):
        current, moving = loop_state
        moving = shifted(moving, "seq", group_size)
        source = (own_group - turn_index) % group_count
        return (absorb(current, moving, valid_for(source), queries, head_count), moving)

    carried, key_value = lax.fori_loop(1, group_count, one_turn, (carried, key_value))
    running, denominator, numerator = carried
    attended = (numerator / denominator[:, :, None]).astype(jnp.bfloat16).reshape(query_count, -1)
    attended = ungroup(attended, bit_count)
    got_prev, got_next = pass_strips(attended.reshape(ROWS_DEV, WCOLS, -1))
    projected = project_rows(attended, w_out)
    from_prev = project_rows(got_prev, w_out)
    from_next = project_rows(got_next, w_out)
    weight_own = blend[0].reshape(ROWS_DEV, WCOLS, 1).astype(jnp.float32)
    partner = jnp.concatenate([from_prev, from_next], axis=1).astype(jnp.float32)
    joined = (
        weight_own * projected.astype(jnp.float32) + (blend_total - weight_own) * partner
    ) / blend_total
    return joined.astype(jnp.bfloat16).reshape(1, -1, joined.shape[-1])


def solution(mesh):
    placed = (
        P(("pano", "win"), "seq", None),
        P(("pano", "win"), "seq", None),
        P(("pano", "win"), "seq", None),
        P(("pano", "win"), "seq", None),
        P(("pano", "win"), "seq", None),
        P(("pano", "win"), None),
        P(("pano", "win"), "seq"),
        P(),
    )
    return jax.shard_map(
        on_device,
        mesh=mesh,
        in_specs=placed,
        out_specs=P(("pano", "win"), "seq", None),
        check_vma=False,
    )
```

profile of v0, /device:TPU:1, one launch (start us, length us, event | category | flops | bytes accessed | tf_op | source)
XLA Modules:
  0.0 136.6 jit_solution(3077362369434255031)
XLA Ops:
  0.0 1.9 %concatenate.28 = bf16[192,2,2,384]{3,2,1,0:T(2,128)(2,1)S(1)} reshape(bf16[1,192,1536]{2,1,0:T(8,128)(2,1)} %param.8) | data formatting | bytes 1179648 | tf_op jit(solution)/shard_map/concatenate | solution.py:105
  2.0 0.4 constant_dynamic-update-slice_fusion.4
  2.4 1.9 %concatenate.29 = bf16[192,2,2,384]{3,2,1,0:T(2,128)(2,1)S(1)} reshape(bf16[1,192,1536]{2,1,0:T(8,128)(2,1)} %param.9) | data formatting | bytes 1179648 | tf_op jit(solution)/shard_map/concatenate | solution.py:105
  4.4 1.9 %concatenate.31 = bf16[192,2,2,384]{3,2,1,0:T(2,128)(2,1)S(1)} reshape(bf16[1,192,1536]{2,1,0:T(8,128)(2,1)} %param.10) | data formatting | bytes 1179648 | tf_op jit(solution)/shard_map/concatenate | solution.py:105
  6.4 0.5 constant_dynamic-update-slice_fusion.3
  7.0 0.5 constant_dynamic-update-slice_fusion.1
  7.6 5.1 %constant_dynamic-slice_fusion.3 = (bf16[608,2,1,384]{3,2,1,0:T(2,128)(2,1)}, bf16[608,2,1,384]{3,2,1,0:T(2,128)(2,1)S(1)}) fusion(bf16[608,2,2,384]{3,2,1,0:T(2,128)(2,1)S(1)} %constant_dynamic-update-slice_fusion, s32[]{:T(128)S(6)} %select_n.83, s32[]{:T(128)S(6)} %select_n.84), kind=kLoop, calls=%fused_computation.60 | loop fusion | bytes 3735560 | tf_op jit(solution)/shard_map/jit(dynamic_index_in_dim)/dynamic_slice | solution.py:39
  12.7 0.1 copy.52
  12.8 2.2 %collective-permute-start = (bf16[608,2,384]{2,0,1:T(8,128)(2,1)S(1)}, bf16[608,2,384]{2,0,1:T(8,128)(2,1)S(1)}, u32[]{:S(2)}, u32[]{:S(2)}) collective-permute-start(bf16[608,2,384]{2,0,1:T(8,128)(2,1)S(1)} %bitcast.75), channel_id=1, source_target_pairs={{0,4},{4,0},{8,12},{12,8},{1,5},{5,1},{9,13},{13,9},{2,6},{6,2},{1... | collective-permute-start | bytes 2801672 | tf_op jit(solution)/shard_map/ppermute | solution.py:23
  15.0 20.4 %collective-permute-done = bf16[608,2,384]{2,0,1:T(8,128)(2,1)S(1)} collective-permute-done((bf16[608,2,384]{2,0,1:T(8,128)(2,1)S(1)}, bf16[608,2,384]{2,0,1:T(8,128)(2,1)S(1)}, u32[]{:S(2)}, u32[]{:S(2)}) %collective-permute-start) | collective-permute-done | bytes 933920 | tf_op jit(solution)/shard_map/ppermute | solution.py:23
  35.4 1.8 %bitcast_select_fusion = (bf16[608,2,384]{2,0,1:T(8,128)(2,1)S(1)}, bf16[608,2,384]{2,0,1:T(8,128)(2,1)S(1)}) fusion(bf16[608,2,384]{2,0,1:T(8,128)(2,1)S(1)} %collective-permute-done, pred[]{:T(512)S(6)} %eq.4, bf16[608,2,1,384]{3,2,1,0:T(2,128)(2,1)} %get-tuple-element.11), kind=kLoop, calls=%fused_computation.29 | loop fusion | flops 933888 | bytes 3735553 | tf_op jit(solution)/shard_map/jit(_where)/select_n | solution.py:43
  37.2 1.0 fusion.18
  38.2 2.2 %collective-permute-start.1 = (bf16[1216,1,384]{2,0,1:T(8,128)(2,1)}, bf16[1216,1,384]{2,0,1:T(8,128)(2,1)S(1)}, u32[]{:S(2)}, u32[]{:S(2)}) collective-permute-start(bf16[1216,1,384]{2,0,1:T(8,128)(2,1)} %fusion.18), channel_id=1, source_target_pairs={{0,8},{8,0},{4,12},{12,4},{1,9},{9,1},{5,13},{13,5},{2,10},{10,2},... | collective-permute-start | bytes 2801672 | tf_op jit(solution)/shard_map/ppermute | solution.py:23
  40.5 0.1 ne.15
  40.5 0.1 concatenate.27
  40.6 0.1 broadcast_in_dim.26
  40.7 40.4 %collective-permute-done.1 = bf16[1216,1,384]{2,0,1:T(8,128)(2,1)S(1)} collective-permute-done((bf16[1216,1,384]{2,0,1:T(8,128)(2,1)}, bf16[1216,1,384]{2,0,1:T(8,128)(2,1)S(1)}, u32[]{:S(2)}, u32[]{:S(2)}) %collective-permute-start.1) | collective-permute-done | bytes 933920 | tf_op jit(solution)/shard_map/ppermute | solution.py:23
  81.1 0.4 broadcast_select_fusion.1
  81.5 0.2 pad_maximum_fusion
  81.7 0.1 fusion.33
  81.8 0.1 slice.21
  81.9 0.2 reshape.85
  82.1 0.2 reshape.79
  82.3 1.3 bitcast_reduce_fusion
  83.7 2.2 %fusion.1 = f32[768,3]{0,1:T(4,128)S(1)} fusion(f32[3,832,768]{2,1,0:T(8,128)S(1)} %get-tuple-element.24, f32[768,3]{0,1:T(4,128)S(1)} %get-tuple-element.23, pred[832]{0:T(1024)(128)(4,1)S(1)} %broadcast_in_dim.26), kind=kLoop, calls=%fused_computation.4 | loop fusion | flops 7665408 | bytes 7686976 | tf_op jit(solution)/shard_map/reduce_sum | solution.py:75
  85.9 0.8 copy-done
  86.7 0.2 reshape.86
  86.9 5.1 %divide_convert_fusion = bf16[768,3,128]{0,2,1:T(8,128)(2,1)S(1)} fusion(f32[3,832,768]{2,1,0:T(8,128)} %copy-done, f32[768,3]{0,1:T(4,128)S(1)} %get-tuple-element.23, pred[832]{0:T(1024)(128)(4,1)S(1)} %broadcast_in_dim.26, bf16[832,3,128]{2,1,0:T(4,128)(2,1)S(1)} %reshape.86, f32[768,3]{0,1:T(4,128)S(1)} %get-tuple-element.22, ...), kind=kOutput, calls=%fused_computation.26 | convolution fusion | flops 499286016 | bytes 8924992 | tf_op jit(solution)/shard_map/qhk,khd->qhd/dot_general | solution.py:76
  92.1 0.1 reshape_reshape_reshape.6
  92.2 1.2 constant_dynamic-slice_fusion.1
  93.4 0.9 copy.38
  94.3 0.1 collective-permute-start.2
  94.4 0.9 copy.37
  95.2 13.6 %collective-permute-done.2 = bf16[384,1,384]{2,0,1:T(8,128)(2,1)S(1)} collective-permute-done((bf16[384,1,384]{2,0,1:T(8,128)(2,1)S(1)}, bf16[384,1,384]{2,0,1:T(8,128)(2,1)S(1)}, u32[]{:S(2)}, u32[]{:S(2)}) %collective-permute-start.2) | collective-permute-done | bytes 294944 | tf_op jit(solution)/shard_map/ppermute | solution.py:23
  109.0 0.1 collective-permute-start.3
  109.0 6.4 %collective-permute-done.3 = bf16[192,2,384]{2,0,1:T(8,128)(2,1)S(1)} collective-permute-done((bf16[192,2,384]{2,0,1:T(8,128)(2,1)S(1)}, bf16[192,2,384]{2,0,1:T(8,128)(2,1)S(1)}, u32[]{:S(2)}, u32[]{:S(2)}) %collective-permute-start.3) | collective-permute-done | bytes 294944 | tf_op jit(solution)/shard_map/ppermute | solution.py:23
  115.4 0.1 select_bitcast_fusion.1
  115.5 0.1 pad_maximum_fusion.2
  115.6 0.6 copy.27
  116.2 0.4 reshape_reshape_reshape.7
  116.7 3.7 %collective-permute-start.4 = (bf16[3,32,1536]{2,1,0:T(8,128)(2,1)S(1)}, bf16[3,32,1536]{2,1,0:T(8,128)(2,1)S(1)}, u32[]{:S(2)}, u32[]{:S(2)}) collective-permute-start(bf16[3,32,1536]{2,1,0:T(8,128)(2,1)S(1)} %get-tuple-element.15), channel_id=1, source_target_pairs={{3,0},{0,1},{1,2},{2,3},{7,4},{4,5},{5,6},{6,7},{11,8},{8,9},{9,10... | collective-permute-start | bytes 884744 | tf_op jit(solution)/shard_map/ppermute | solution.py:29
  120.4 0.4 reshape_reshape.9
  120.8 4.6 %collective-permute-done.4 = bf16[3,32,1536]{2,1,0:T(8,128)(2,1)S(1)} collective-permute-done((bf16[3,32,1536]{2,1,0:T(8,128)(2,1)S(1)}, bf16[3,32,1536]{2,1,0:T(8,128)(2,1)S(1)}, u32[]{:S(2)}, u32[]{:S(2)}) %collective-permute-start.4) | collective-permute-done | bytes 294944 | tf_op jit(solution)/shard_map/ppermute | solution.py:29
  125.5 5.4 %convolution_convert_fusion.2 = bf16[96,3072]{1,0:T(8,128)(2,1)S(1)} fusion(bf16[96,1536]{1,0:T(8,128)(2,1)S(1)} %bitcast.76, bf16[1536,3072]{1,0:T(8,128)(2,1)} %param.15), kind=kOutput, calls=%fused_computation.16 | convolution fusion | flops 906264576 | bytes 10321920 | tf_op jit(solution)/shard_map/dot_general | solution.py:94
  131.0 0.7 slice-done.2
  131.6 1.7 %convolution_convert_fusion.1 = bf16[96,3072]{1,0:T(8,128)(2,1)S(1)} fusion(bf16[96,1536]{1,0:T(8,128)(2,1)S(1)} %bitcast.77, bf16[1536,3072]{1,0:T(8,128)(2,1)S(1)} %bitcast.65), kind=kOutput, calls=%fused_computation.15 | convolution fusion | flops 906264576 | bytes 10321920 | tf_op jit(solution)/shard_map/dot_general | solution.py:94
  133.4 0.1 pad_maximum_fusion.1
  133.5 3.2 %fusion.11 = bf16[1,192,3072]{2,1,0:T(8,128)(2,1)} fusion(bf16[192,1536]{1,0:T(8,128)(2,1)S(1)} %reshape_reshape.9, bf16[1536,3072]{1,0:T(8,128)(2,1)S(1)} %bitcast.65, bf16[192,3072]{1,0:T(8,128)(2,1)S(1)} %bitcast.74, f32[192]{0:T(256)S(1)} %broadcast_subtract_fusion, f32[192]{0:T(256)S(1)} %bitcast.80), kind=kOutput, calls=%fused_computation.14 | convolution fusion | flops 1816657920 | bytes 12387840 | tf_op jit(solution)/shard_map/dot_general | solution.py:94
  (28 shorter events, 0.4 us)
Async XLA Ops:
  0.0 4.3 %copy-start.1 = (bf16[1,16,1536]{2,1,0:T(8,128)(2,1)S(1)}, bf16[1,16,1536]{2,1,0:T(8,128)(2,1)}, u32[]{:S(2)}) copy-start(bf16[1,16,1536]{2,1,0:T(8,128)(2,1)} %param.11) | copy-start | bytes 147460
  2.0 4.4 %copy-start.2 = (bf16[1,16,1536]{2,1,0:T(8,128)(2,1)S(1)}, bf16[1,16,1536]{2,1,0:T(8,128)(2,1)}, u32[]{:S(2)}) copy-start(bf16[1,16,1536]{2,1,0:T(8,128)(2,1)} %param.12) | copy-start | bytes 147460
  12.8 22.6 %collective-permute-start = (bf16[608,2,384]{2,0,1:T(8,128)(2,1)S(1)}, bf16[608,2,384]{2,0,1:T(8,128)(2,1)S(1)}, u32[]{:S(2)}, u32[]{:S(2)}) collective-permute-start(bf16[608,2,384]{2,0,1:T(8,128)(2,1)S(1)} %bitcast.75), channel_id=1, source_target_pairs={{0,4},{4,0},{8,12},{12,8},{1,5},{5,1},{9,13},{13,9},{2,6},{6,2},{1... | collective-permute-start | bytes 2801672 | tf_op jit(solution)/shard_map/ppermute | solution.py:23
  37.2 3.2 %copy-start.4 = (s32[1,64]{1,0:T(1,128)S(1)}, s32[1,64]{1,0:T(1,128)}, u32[]{:S(2)}) copy-start(s32[1,64]{1,0:T(1,128)} %param.13) | copy-start | bytes 772
  38.2 42.8 %collective-permute-start.1 = (bf16[1216,1,384]{2,0,1:T(8,128)(2,1)}, bf16[1216,1,384]{2,0,1:T(8,128)(2,1)S(1)}, u32[]{:S(2)}, u32[]{:S(2)}) collective-permute-start(bf16[1216,1,384]{2,0,1:T(8,128)(2,1)} %fusion.18), channel_id=1, source_target_pairs={{0,8},{8,0},{4,12},{12,4},{1,9},{9,1},{5,13},{13,5},{2,10},{10,2},... | collective-permute-start | bytes 2801672 | tf_op jit(solution)/shard_map/ppermute | solution.py:23
  83.7 3.0 %copy-start = (f32[3,832,768]{2,1,0:T(8,128)}, f32[3,832,768]{2,1,0:T(8,128)S(1)}, u32[]{:S(2)}) copy-start(f32[3,832,768]{2,1,0:T(8,128)S(1)} %get-tuple-element.24) | copy-start | bytes 23003140
  94.3 14.6 %collective-permute-start.2 = (bf16[384,1,384]{2,0,1:T(8,128)(2,1)S(1)}, bf16[384,1,384]{2,0,1:T(8,128)(2,1)S(1)}, u32[]{:S(2)}, u32[]{:S(2)}) collective-permute-start(bf16[384,1,384]{2,0,1:T(8,128)(2,1)S(1)} %bitcast.78), channel_id=1, source_target_pairs={{0,8},{8,0},{4,12},{12,4},{1,9},{9,1},{5,13},{13,5},{2,10},{10,2},... | collective-permute-start | bytes 884744 | tf_op jit(solution)/shard_map/ppermute | solution.py:23
  109.0 6.5 %collective-permute-start.3 = (bf16[192,2,384]{2,0,1:T(8,128)(2,1)S(1)}, bf16[192,2,384]{2,0,1:T(8,128)(2,1)S(1)}, u32[]{:S(2)}, u32[]{:S(2)}) collective-permute-start(bf16[192,2,384]{2,0,1:T(8,128)(2,1)S(1)} %fusion.27), channel_id=1, source_target_pairs={{0,4},{4,0},{8,12},{12,8},{1,5},{5,1},{9,13},{13,9},{2,6},{6,2},{1... | collective-permute-start | bytes 884744 | tf_op jit(solution)/shard_map/ppermute | solution.py:23
  115.6 4.8 %copy-start.3 = (s32[1,192]{1,0:T(1,128)S(1)}, s32[1,192]{1,0:T(1,128)}, u32[]{:S(2)}) copy-start(s32[1,192]{1,0:T(1,128)} %param.14) | copy-start | bytes 2308
  116.7 8.8 %collective-permute-start.4 = (bf16[3,32,1536]{2,1,0:T(8,128)(2,1)S(1)}, bf16[3,32,1536]{2,1,0:T(8,128)(2,1)S(1)}, u32[]{:S(2)}, u32[]{:S(2)}) collective-permute-start(bf16[3,32,1536]{2,1,0:T(8,128)(2,1)S(1)} %get-tuple-element.15), channel_id=1, source_target_pairs={{3,0},{0,1},{1,2},{2,3},{7,4},{4,5},{5,6},{6,7},{11,8},{8,9},{9,10... | collective-permute-start | bytes 884744 | tf_op jit(solution)/shard_map/ppermute | solution.py:29
  120.4 10.6 %slice-start = ((s8[9437184]{0:T(1024)(128)(4,1)}), s8[1048576]{0:T(1024)(128)(4,1)S(1)}, s32[]{:S(2)}) async-start(s8[9437184]{0:T(1024)(128)(4,1)} %bitcast.64), calls=%async_computation | async-start | bytes 2097152
  120.8 10.2 %collective-permute-start.5 = (bf16[3,32,1536]{2,1,0:T(8,128)(2,1)S(1)}, bf16[3,32,1536]{2,1,0:T(8,128)(2,1)S(1)}, u32[]{:S(2)}, u32[]{:S(2)}) collective-permute-start(bf16[3,32,1536]{2,1,0:T(8,128)(2,1)S(1)} %get-tuple-element.16), channel_id=1, source_target_pairs={{1,0},{2,1},{3,2},{0,3},{5,4},{6,5},{7,6},{4,7},{9,8},{10,9},{11,1... | collective-permute-start | bytes 884744 | tf_op jit(solution)/shard_map/ppermute | solution.py:29
  125.5 5.5 %slice-start.1 = ((s8[9437184]{0:T(1024)(128)(4,1)}), s8[4194304]{0:T(1024)(128)(4,1)S(1)}, s32[]{:S(2)}) async-start(s8[9437184]{0:T(1024)(128)(4,1)} %bitcast.64), calls=%async_computation.1 | async-start | bytes 8388608
  125.5 6.1 %slice-start.2 = ((s8[9437184]{0:T(1024)(128)(4,1)}), s8[4194304]{0:T(1024)(128)(4,1)S(1)}, s32[]{:S(2)}) async-start(s8[9437184]{0:T(1024)(128)(4,1)} %bitcast.64), calls=%async_computation.2 | async-start | bytes 8388608
where the time goes:
time: 139 us; the launch traced here: 137 us
  waiting for transfers between devices  85.4 us (61%)
  local copies, waits for them, and re-layouts  19.8 us (14%)
  matrix products  16.8 us (12%)
  starting transfers between devices  8.29 us (6%)
  other arithmetic  5.97 us (4%)
    ppermute x4, waiting for transfers between devices, swapped(): return lax.ppermute(block, axis, route)  80.8 us
    dot_general x3, matrix products, project_rows(): jnp.dot(flat_rows, w_out, preferred_element_type=jnp.float32)  10.3 us
    concatenate x6, local copies, waits for them, and re-layouts, on_device(): jnp.concatenate([query[0], key_image[0], key_text[0], value_image[0], val...  5.93 us
    dot_general x1, matrix products, absorb(): jnp.einsum('qhk,khd->qhd', weights.astype(jnp.bfloat16), values_block, pr...  5.15 us
    dynamic_slice x1, local copies, waits for them, and re-layouts, regroup(): kept_half = lax.dynamic_index_in_dim(paired, own_bit, 2, keepdims=False)  5.11 us
    unnamed x22, local copies, waits for them, and re-layouts  4.71 us
    ppermute x2, waiting for transfers between devices, shifted(): return lax.ppermute(block, axis, route)  4.65 us
    ppermute x4, starting transfers between devices, swapped(): return lax.ppermute(block, axis, route)  4.51 us
  transfers between devices with their start and end apart: 6, of which 5 were waited for; matrix products, arithmetic and copies ran while one was open for 5% of the time, Pallas kernels for 0%

commit v1 on v0

--- a/solution.py
+++ b/solution.py
@@ -1,6 +1,10 @@
+import functools
+
 import jax
 import jax.numpy as jnp
 from jax import lax
+from jax.experimental import pallas as pl
+from jax.experimental.pallas import tpu as pltpu
 from jax.sharding import PartitionSpec as P
 
 HEADS = 12
@@ -149,7 +153,273 @@
     return joined.astype(jnp.bfloat16).reshape(1, -1, joined.shape[-1])
 
 
+MESH = pl.DeviceIdType.MESH
+LOG2E = 1.4426950408889634
+
+
+def partner_of(position, mask):
+    bit = 1
+    while bit <= mask:
+        if mask & bit:
+            position = position + (1 - 2 * ((position // bit) % 2)) * bit
+        bit *= 2
+    return position
+
+
+def attend_kernel(
+    count, rounds, query, key_image, key_text, value_image, value_text, prompt_ids, blend,
+    out, queries, keys, values, left, right, prev_right, mixed, blends,
+    send_sem, recv_sem, own_sem, blend_send, blend_recv, strip_send, strip_recv,
+    back_send, back_recv, back_own, pass_send, pass_recv,
+):
+    image_rows = query.shape[1]
+    text_rows = key_text.shape[1]
+    all_image = count * image_rows
+    strip_rows = image_rows // WCOLS
+    pad_rows = keys.shape[1] - all_image - count * text_rows
+    me = lax.axis_index("seq")
+    windows = lax.axis_size("win")
+    window = lax.axis_index("win")
+    after = lax.rem(window + 1, windows)
+    before = lax.rem(window + windows - 1, windows)
+    masks = list(range(count - 1, 0, -1))
+
+    barrier = pltpu.get_barrier_semaphore()
+    for mask in masks:
+        pl.semaphore_signal(barrier, inc=1, device_id={"seq": partner_of(me, mask)}, device_id_type=MESH)
+    for other in (after, before):
+        pl.semaphore_signal(barrier, inc=1, device_id={"win": other}, device_id_type=MESH)
+
+    blends[me] = jnp.broadcast_to(blend[...].astype(jnp.float32), (8, image_rows))
+    if pad_rows:
+        zeros = jnp.zeros((rounds, pad_rows, HEAD_DIM), keys.dtype)
+        keys[:, all_image + count * text_rows :, :] = zeros
+        values[:, all_image + count * text_rows :, :] = zeros
+
+    def pieces(turn, head, place):
+        columns = pl.ds(pl.multiple_of(head * HEAD_DIM, HEAD_DIM), HEAD_DIM)
+        image = pl.ds(pl.multiple_of(place * image_rows, image_rows), image_rows)
+        text = pl.ds(pl.multiple_of(all_image + place * text_rows, text_rows), text_rows)
+        return (
+            (query.at[0, :, columns], queries.at[turn, image, :]),
+            (key_image.at[0, :, columns], keys.at[turn, image, :]),
+            (key_text.at[0, :, columns], keys.at[turn, text, :]),
+            (value_image.at[0, :, columns], values.at[turn, image, :]),
+            (value_text.at[0, :, columns], values.at[turn, text, :]),
+        )
+
+    def sends(turn, place_of=None):
+        made = []
+        for mask in masks:
+            other = partner_of(me, mask)
+            place = me if place_of is None else other
+            for index, (source, target) in enumerate(pieces(turn, turn * count + other, place)):
+                made.append(pltpu.make_async_remote_copy(
+                    source, target, send_sem.at[turn, mask - 1, index], recv_sem.at[turn, mask - 1, index],
+                    device_id={"seq": other}, device_id_type=MESH))
+        return made
+
+    def owns(turn):
+        return [
+            pltpu.make_async_copy(source, target, own_sem.at[turn, index])
+            for index, (source, target) in enumerate(pieces(turn, turn * count + me, me))
+        ]
+
+    def blend_copies(place_of=None):
+        made = []
+        for mask in masks:
+            other = partner_of(me, mask)
+            place = me if place_of is None else other
+            made.append(pltpu.make_async_remote_copy(
+                blends.at[place], blends.at[place], blend_send.at[mask - 1], blend_recv.at[mask - 1],
+                device_id={"seq": other}, device_id_type=MESH))
+        return made
+
+    def strip_copy(turn):
+        return pltpu.make_async_remote_copy(
+            right.at[turn], prev_right.at[turn], strip_send.at[turn], strip_recv.at[turn],
+            device_id={"win": after}, device_id_type=MESH)
+
+    def back_columns(turn, place):
+        return pl.ds(pl.multiple_of((turn * count + place) * HEAD_DIM, HEAD_DIM), HEAD_DIM)
+
+    def back_copies(turn, place_of=None):
+        made = []
+        for mask in masks:
+            other = partner_of(me, mask)
+            place = me if place_of is None else other
+            made.append(pltpu.make_async_remote_copy(
+                mixed.at[turn, pl.ds(other * strip_rows, strip_rows)],
+                out.at[:, 0, :, back_columns(turn, place)],
+                back_send.at[turn, mask - 1], back_recv.at[turn, mask - 1],
+                device_id={"seq": other}, device_id_type=MESH))
+        return made
+
+    def back_local(turn):
+        return pltpu.make_async_copy(
+            mixed.at[turn, pl.ds(me * strip_rows, strip_rows)],
+            out.at[:, 0, :, back_columns(turn, me)], back_own.at[turn])
+
+    def pass_copy(turn):
+        width = count * HEAD_DIM
+        columns = pl.ds(pl.multiple_of(turn * width, width), width)
+        return pltpu.make_async_remote_copy(
+            out.at[:, 0, :, columns], out.at[:, 1, :, columns], pass_send.at[turn], pass_recv.at[turn],
+            device_id={"win": before}, device_id_type=MESH)
+
+    for turn in range(rounds):
+        for copy in owns(turn):
+            copy.start()
+    pl.semaphore_wait(barrier, len(masks) + 2)
+    for copy in blend_copies():
+        copy.start()
+    for turn in range(min(2, rounds)):
+        for copy in sends(turn):
+            copy.start()
+
+    text_width = keys.shape[1] - all_image
+    given = jnp.where(prompt_ids[...] != 0, 0.0, -jnp.inf).astype(jnp.float32)
+    if pad_rows:
+        given = jnp.concatenate([given, jnp.full((1, pad_rows), -jnp.inf, jnp.float32)], axis=1)
+    scale = HEAD_DIM ** -0.5 * LOG2E
+    token = lax.broadcasted_iota(jnp.int32, (strip_rows * STRIDE, image_rows), 1)
+    spot = lax.broadcasted_iota(jnp.int32, (strip_rows * STRIDE, image_rows), 0)
+    chosen = token == (spot // STRIDE) * WCOLS + spot % STRIDE
+    contract = (((1,), (1,)), ((), ()))
+
+    def one_round(turn, carry):
+        for copy in sends(turn, 1):
+            copy.wait_recv()
+        for copy in owns(turn):
+            copy.wait()
+
+        def one_block(block, carry):
+            rows = pl.ds(pl.multiple_of(block * image_rows, image_rows), image_rows)
+            held = queries[turn, rows, :]
+            image_scores = lax.dot_general(held, keys[turn, :all_image, :], contract, preferred_element_type=jnp.float32)
+            text_scores = lax.dot_general(held, keys[turn, all_image:, :], contract, preferred_element_type=jnp.float32) + given
+            peak = jnp.maximum(jnp.max(image_scores, axis=1, keepdims=True), jnp.max(text_scores, axis=1, keepdims=True))
+            image_weights = jnp.exp2((image_scores - peak) * scale)
+            text_weights = jnp.exp2((text_scores - peak) * scale)
+            total = jnp.sum(image_weights, axis=1, keepdims=True) + jnp.sum(text_weights, axis=1, keepdims=True)
+            product = jnp.dot(image_weights.astype(jnp.bfloat16), values[turn, :all_image, :], preferred_element_type=jnp.float32)
+            product += jnp.dot(text_weights.astype(jnp.bfloat16), values[turn, all_image:, :], preferred_element_type=jnp.float32)
+            attended = (product * (1.0 / total)).astype(jnp.bfloat16).reshape(strip_rows, WCOLS, HEAD_DIM)
+            window_rows = pl.ds(block * strip_rows, strip_rows)
+            left[turn, window_rows] = attended[:, :STRIDE]
+            right[turn, window_rows] = attended[:, STRIDE:]
+            return carry
+
+        lax.fori_loop(0, count, one_block, 0)
+        strip_copy(turn).start()
+
+        @pl.when(turn == 0)
+        def _():
+            for copy in blend_copies(1):
+                copy.wait_recv()
+
+        strip_copy(turn).wait_recv()
+
+        def one_mix(block, carry):
+            window_rows = pl.ds(block * strip_rows, strip_rows)
+            spread = jnp.where(chosen, blends[block][:1, :], 0.0).astype(jnp.bfloat16)
+            own = jnp.dot(spread, jnp.ones((image_rows, HEAD_DIM), jnp.bfloat16), preferred_element_type=jnp.float32)
+            own = own.reshape(strip_rows, STRIDE, HEAD_DIM)
+            mine = left[turn, window_rows].astype(jnp.float32)
+            theirs = prev_right[turn, window_rows].astype(jnp.float32)
+            mixed[turn, window_rows] = ((own * mine + (blend_total - own) * theirs) * (1.0 / blend_total)).astype(jnp.bfloat16)
+            return carry
+
+        lax.fori_loop(0, count, one_mix, 0)
+        for copy in back_copies(turn):
+            copy.start()
+        back_local(turn).start()
+
+        @pl.when(turn + 2 < rounds)
+        def _():
+            for copy in sends(turn + 2):
+                copy.start()
+
+        return carry
+
+    lax.fori_loop(0, rounds, one_round, 0)
+
+    def one_pass(turn, carry):
+        for copy in back_copies(turn, 1):
+            copy.wait_recv()
+        back_local(turn).wait()
+        pass_copy(turn).start()
+        return carry
+
+    lax.fori_loop(0, rounds, one_pass, 0)
+
+    def finish(turn, carry):
+        for copy in sends(turn) + back_copies(turn):
+            copy.wait_send()
+        strip_copy(turn).wait_send()
+        pass_copy(turn).wait()
+        return carry
+
+    lax.fori_loop(0, rounds, finish, 0)
+    for copy in blend_copies():
+        copy.wait_send()
+
+
+def attend_in_kernel(count, query, key_image, value_image, key_text, value_text, prompt_ids, blend):
+    image_rows, text_rows = query.shape[1], key_text.shape[1]
+    rounds = query.shape[2] // HEAD_DIM // count
+    all_image = count * image_rows
+    key_rows = all_image + -(-count * text_rows // 128) * 128
+    strip_rows = image_rows // WCOLS
+    window_strip = (rounds, count * strip_rows, STRIDE, HEAD_DIM)
+    anywhere = pl.BlockSpec(memory_space=pl.ANY)
+    vmem = pl.BlockSpec(memory_space=pltpu.VMEM)
+    dma = pltpu.SemaphoreType.DMA
+    out = pl.pallas_call(
+        functools.partial(attend_kernel, count, rounds),
+        out_shape=jax.ShapeDtypeStruct((strip_rows, 2, STRIDE, query.shape[2]), jnp.bfloat16),
+        in_specs=[anywhere] * 5 + [vmem] * 2,
+        out_specs=anywhere,
+        scratch_shapes=[
+            pltpu.VMEM((rounds, all_image, HEAD_DIM), jnp.bfloat16),
+            pltpu.VMEM((rounds, key_rows, HEAD_DIM), jnp.bfloat16),
+            pltpu.VMEM((rounds, key_rows, HEAD_DIM), jnp.bfloat16),
+            pltpu.VMEM(window_strip, jnp.bfloat16),
+            pltpu.VMEM(window_strip, jnp.bfloat16),
+            pltpu.VMEM(window_strip, jnp.bfloat16),
+            pltpu.VMEM(window_strip, jnp.bfloat16),
+            pltpu.VMEM((count, 8, image_rows), jnp.float32),
+            dma((rounds, count - 1, 5)),
+            dma((rounds, count - 1, 5)),
+            dma((rounds, 5)),
+            dma((count - 1,)),
+            dma((count - 1,)),
+            dma((rounds,)),
+            dma((rounds,)),
+            dma((rounds, count - 1)),
+            dma((rounds, count - 1)),
+            dma((rounds,)),
+            dma((rounds,)),
+            dma((rounds,)),
+        ],
+        compiler_params=pltpu.CompilerParams(
+            collective_id=0, has_side_effects=True, vmem_limit_bytes=32 * 1024 * 1024
+        ),
+    )(query, key_image, key_text, value_image, value_text, prompt_ids, blend)
+    return out.reshape(image_rows, query.shape[2])
+
+
+def on_device_by_heads(query, key_image, value_image, key_text, value_text, prompt_ids, blend, w_out):
+    blended = attend_in_kernel(
+        lax.axis_size("seq"), query, key_image, value_image, key_text, value_text, prompt_ids, blend
+    )
+    joined = jnp.dot(blended, w_out, preferred_element_type=jnp.float32).astype(jnp.bfloat16)
+    return joined[None]
+
+
 def solution(mesh):
+    seq_count = mesh.shape["seq"]
+    by_heads = seq_count > 1 and seq_count & (seq_count - 1) == 0 and HEADS % seq_count == 0
     placed = (
         P(("pano", "win"), "seq", None),
         P(("pano", "win"), "seq", None),
@@ -161,7 +431,7 @@
         P(),
     )
     return jax.shard_map(
-        on_device,
+        on_device_by_heads if by_heads else on_device,
         mesh=mesh,
         in_specs=placed,
         out_specs=P(("pano", "win"), "seq", None),

time: 139 us -> 76.9 us (0.55); the launches traced: 137 us -> 76.5 us
  waiting for transfers between devices: 85.4 us -> 0 us
  Pallas kernels: 0 us -> 63.7 us
  local copies, waits for them, and re-layouts: 19.8 us -> 6.12 us
  matrix products: 16.8 us -> 6.7 us
  starting transfers between devices: 8.29 us -> 0 us
  other arithmetic: 5.97 us -> 0 us
    ppermute x6 -> x0, waiting for transfers between devices: 85.4 us -> none  [the longest x4 80.8 us: swapped(): return lax.ppermute(block, axis, route)]
    pallas_call x0 -> x1, Pallas kernels: none -> 63.7 us  [attend_in_kernel(): pl.pallas_call(functools.partial(attend_kernel, count, rounds), out_shape...]
    dot_general x5 -> x1, matrix products: 16.8 us -> 6.7 us  [on_device_by_heads(): jnp.dot(blended, w_out, preferred_element_type=jnp.float32)]
    ppermute x6 -> x0, starting transfers between devices: 8.29 us -> none  [the longest x4 4.51 us: swapped(): return lax.ppermute(block, axis, route)]
    dynamic_slice x3 -> x0, local copies, waits for them, and re-layouts: 6.48 us -> none  [the longest x1 5.11 us: regroup(): kept_half = lax.dynamic_index_in_dim(paired, own_bit, 2, keepdims=False)]
    concatenate x7 -> x0, local copies, waits for them, and re-layouts: 6.01 us -> none  [the longest x6 5.93 us: on_device(): jnp.concatenate([query[0], key_image[0], key_text[0], value_image[0], val...]
    reduce_sum x1 -> x0, other arithmetic: 2.22 us -> none  [absorb(): denominator = denominator * rescale + jnp.sum(weights, axis=2)]
    select_n x3 -> x0, other arithmetic: 2.2 us -> none  [the longest x1 1.77 us: regroup(): upper_half = jnp.where(own_bit == 0, received, kept_half)]
  transfers between devices with their start and end apart: 6 -> 0, of which waited for: 5 -> 0; matrix products, arithmetic and copies ran while one was open for 5% -> 0% of each run, Pallas kernels for 0% -> 0%
where the time goes in v1:
time: 76.9 us; the launch traced here: 76.5 us
  Pallas kernels  63.7 us (83%)
  matrix products  6.7 us (9%)
  local copies, waits for them, and re-layouts  6.12 us (8%)
    pallas_call x1, Pallas kernels, attend_in_kernel(): pl.pallas_call(functools.partial(attend_kernel, count, rounds), out_shape...  63.7 us
    dot_general x1, matrix products, on_device_by_heads(): jnp.dot(blended, w_out, preferred_element_type=jnp.float32)  6.7 us
    unnamed x14, local copies, waits for them, and re-layouts  6.12 us

profile of v1, /device:TPU:1, one launch (start us, length us, event | category | flops | bytes accessed | tf_op | source)
XLA Modules:
  0.0 76.5 jit_solution(14631313652378185387)
XLA Ops:
  0.0 0.0 copy-start
  0.0 1.1 %copy-done = bf16[1,192,1536]{2,1,0:T(8,128)(2,1)S(1)} copy-done((bf16[1,192,1536]{2,1,0:T(8,128)(2,1)S(1)}, bf16[1,192,1536]{2,1,0:T(8,128)(2,1)}, u32[]{:S(2)}) %copy-start) | copy-done | bytes 589848
  1.1 0.0 copy-start.1
  1.1 1.1 %copy-done.1 = bf16[1,192,1536]{2,1,0:T(8,128)(2,1)S(1)} copy-done((bf16[1,192,1536]{2,1,0:T(8,128)(2,1)S(1)}, bf16[1,192,1536]{2,1,0:T(8,128)(2,1)}, u32[]{:S(2)}) %copy-start.1) | copy-done | bytes 589848
  2.1 0.0 copy-start.2
  2.1 1.1 %copy-done.2 = bf16[1,192,1536]{2,1,0:T(8,128)(2,1)S(1)} copy-done((bf16[1,192,1536]{2,1,0:T(8,128)(2,1)S(1)}, bf16[1,192,1536]{2,1,0:T(8,128)(2,1)}, u32[]{:S(2)}) %copy-start.2) | copy-done | bytes 589848
  3.2 0.0 copy-start.3
  3.2 0.8 %copy-done.3 = bf16[1,16,1536]{2,1,0:T(8,128)(2,1)S(1)} copy-done((bf16[1,16,1536]{2,1,0:T(8,128)(2,1)S(1)}, bf16[1,16,1536]{2,1,0:T(8,128)(2,1)}, u32[]{:S(2)}) %copy-start.3) | copy-done | bytes 49176
  4.0 0.0 copy-start.4
  4.0 0.8 %copy-done.4 = bf16[1,16,1536]{2,1,0:T(8,128)(2,1)S(1)} copy-done((bf16[1,16,1536]{2,1,0:T(8,128)(2,1)S(1)}, bf16[1,16,1536]{2,1,0:T(8,128)(2,1)}, u32[]{:S(2)}) %copy-start.4) | copy-done | bytes 49176
  4.8 0.0 copy-start.5
  4.8 0.7 copy-done.5
  5.5 0.0 copy-start.6
  5.5 0.7 copy-done.6
  6.1 63.7 %shard_map.82 = bf16[3,2,32,1536]{3,2,1,0:T(8,128)(2,1)S(1)} custom-call(bf16[1,192,1536]{2,1,0:T(8,128)(2,1)S(1)} %copy-done, bf16[1,192,1536]{2,1,0:T(8,128)(2,1)S(1)} %copy-done.1, bf16[1,16,1536]{2,1,0:T(8,128)(2,1)S(1)} %copy-done.3, bf16[1,192,1536]{2,1,0:T(8,128)(2,1)S(1)} %copy-done.2, bf16[1,16,1536]{2,1,0:T(8,128)(2,1)S(1)} %copy-done.4, ...), custom_call_target="tpu_custom_call" | custom-call | tf_op jit(solution)/shard_map/pallas_call | solution.py:378
  69.8 6.7 %fusion = bf16[1,192,3072]{2,1,0:T(8,128)(2,1)} fusion(bf16[192,1536]{1,0:T(8,128)(2,1)S(1)} %bitcast.5, bf16[1536,3072]{1,0:T(8,128)(2,1)} %param.15), kind=kOutput, calls=%fused_computation.1 | convolution fusion | flops 1812529152 | bytes 11206656 | tf_op jit(solution)/shard_map/dot_general | solution.py:416
Async XLA Ops:
  0.0 1.1 %copy-start = (bf16[1,192,1536]{2,1,0:T(8,128)(2,1)S(1)}, bf16[1,192,1536]{2,1,0:T(8,128)(2,1)}, u32[]{:S(2)}) copy-start(bf16[1,192,1536]{2,1,0:T(8,128)(2,1)} %query.1) | copy-start | bytes 1769476
  1.1 1.1 %copy-start.1 = (bf16[1,192,1536]{2,1,0:T(8,128)(2,1)S(1)}, bf16[1,192,1536]{2,1,0:T(8,128)(2,1)}, u32[]{:S(2)}) copy-start(bf16[1,192,1536]{2,1,0:T(8,128)(2,1)} %key_image.1) | copy-start | bytes 1769476
  2.1 1.1 %copy-start.2 = (bf16[1,192,1536]{2,1,0:T(8,128)(2,1)S(1)}, bf16[1,192,1536]{2,1,0:T(8,128)(2,1)}, u32[]{:S(2)}) copy-start(bf16[1,192,1536]{2,1,0:T(8,128)(2,1)} %value_image.1) | copy-start | bytes 1769476
  3.2 0.8 %copy-start.3 = (bf16[1,16,1536]{2,1,0:T(8,128)(2,1)S(1)}, bf16[1,16,1536]{2,1,0:T(8,128)(2,1)}, u32[]{:S(2)}) copy-start(bf16[1,16,1536]{2,1,0:T(8,128)(2,1)} %key_text.1) | copy-start | bytes 147460
  4.0 0.8 %copy-start.4 = (bf16[1,16,1536]{2,1,0:T(8,128)(2,1)S(1)}, bf16[1,16,1536]{2,1,0:T(8,128)(2,1)}, u32[]{:S(2)}) copy-start(bf16[1,16,1536]{2,1,0:T(8,128)(2,1)} %value_text.1) | copy-start | bytes 147460
  4.8 0.7 copy-start.5
  5.5 0.7 copy-start.6

commit v2 on v0

--- a/solution.py
+++ b/solution.py
@@ -1,6 +1,10 @@
+import functools
+
 import jax
 import jax.numpy as jnp
 from jax import lax
+from jax.experimental import pallas as pl
+from jax.experimental.pallas import tpu as pltpu
 from jax.sharding import PartitionSpec as P
 
 HEADS = 12
@@ -149,7 +153,319 @@
     return joined.astype(jnp.bfloat16).reshape(1, -1, joined.shape[-1])
 
 
+MESH = pl.DeviceIdType.MESH
+LOG2E = 1.4426950408889634
+
+
+VMEM_GRANT = 60 * 1024 * 1024
+
+
+def partner_of(position, mask):
+    bit = 1
+    while bit <= mask:
+        if mask & bit:
+            position = position + (1 - 2 * ((position // bit) % 2)) * bit
+        bit *= 2
+    return position
+
+
+def window_kernel(
+    count, rounds, query, key_image, key_text, value_image, value_text, prompt_ids, blend, w_out,
+    out, queries, keys, values, left, right, prev_right, mixed, blends, features, weights, partial,
+    send_sem, recv_sem, own_sem, blend_send, blend_recv, strip_send, strip_recv,
+    back_send, back_recv, back_own, pass_send, pass_recv, weight_sem,
+):
+    image_rows = query.shape[1]
+    text_rows = key_text.shape[1]
+    all_image = count * image_rows
+    strip_rows = image_rows // WCOLS
+    strip_size = strip_rows * STRIDE
+    pad_rows = keys.shape[1] - all_image - count * text_rows
+    width = count * HEAD_DIM
+    me = lax.axis_index("seq")
+    windows = lax.axis_size("win")
+    window = lax.axis_index("win")
+    after = lax.rem(window + 1, windows)
+    before = lax.rem(window + windows - 1, windows)
+    masks = list(range(count - 1, 0, -1))
+
+    barrier = pltpu.get_barrier_semaphore()
+    for mask in masks:
+        pl.semaphore_signal(barrier, inc=1, device_id={"seq": partner_of(me, mask)}, device_id_type=MESH)
+    for other in (after, before):
+        pl.semaphore_signal(barrier, inc=1, device_id={"win": other}, device_id_type=MESH)
+
+    def pieces(turn, head, place):
+        columns = pl.ds(pl.multiple_of(head * HEAD_DIM, HEAD_DIM), HEAD_DIM)
+        image = pl.ds(pl.multiple_of(place * image_rows, image_rows), image_rows)
+        text = pl.ds(pl.multiple_of(all_image + place * text_rows, text_rows), text_rows)
+        return (
+            (key_image.at[0, :, columns], keys.at[turn, image, :]),
+            (key_text.at[0, :, columns], keys.at[turn, text, :]),
+            (value_image.at[0, :, columns], values.at[turn, image, :]),
+            (value_text.at[0, :, columns], values.at[turn, text, :]),
+            (query.at[0, :, columns], queries.at[turn, image, :]),
+        )
+
+    def moves(turn, mask, arriving=False, indices=range(5)):
+        other = partner_of(me, mask)
+        made = pieces(turn, turn * count + other, other if arriving else me)
+        if mask == 0:
+            return [pltpu.make_async_copy(s, t, own_sem.at[turn, i]) for i, (s, t) in enumerate(made) if i in indices]
+        return [
+            pltpu.make_async_remote_copy(
+                s, t, send_sem.at[turn, mask - 1, i], recv_sem.at[turn, mask - 1, i],
+                device_id={"seq": other}, device_id_type=MESH)
+            for i, (s, t) in enumerate(made)
+            if i in indices
+        ]
+
+    def send_keys(turn):
+        for index in range(4):
+            for mask in masks:
+                moves(turn, mask, indices=[index])[0].start()
+
+    def send_queries(turn):
+        for mask in masks:
+            moves(turn, mask, indices=[4])[0].start()
+
+    def arrived(turn, mask, indices):
+        for copy in moves(turn, mask, True, indices):
+            if mask == 0:
+                copy.wait()
+            else:
+                copy.wait_recv()
+
+    def blend_copy(mask, arriving=False):
+        other = partner_of(me, mask)
+        place = other if arriving else me
+        return pltpu.make_async_remote_copy(
+            blends.at[place], blends.at[place], blend_send.at[mask - 1], blend_recv.at[mask - 1],
+            device_id={"seq": other}, device_id_type=MESH)
+
+    def strip_place(mask):
+        place = partner_of(me, mask)
+        return pl.ds(pl.multiple_of(place * strip_size, strip_size), strip_size)
+
+    def strip_copy(turn, mask):
+        rows = strip_place(mask)
+        return pltpu.make_async_remote_copy(
+            right.at[turn, rows], prev_right.at[turn, rows], strip_send.at[turn, mask], strip_recv.at[turn, mask],
+            device_id={"win": after}, device_id_type=MESH)
+
+    def head_columns(turn, place):
+        return pl.ds(pl.multiple_of((turn * count + place) * HEAD_DIM, HEAD_DIM), HEAD_DIM)
+
+    def back_copy(turn, mask, arriving=False):
+        other = partner_of(me, mask)
+        source = mixed.at[turn, strip_place(mask)]
+        target = features.at[0, :, head_columns(turn, other if arriving else me)]
+        if mask == 0:
+            return pltpu.make_async_copy(source, target, back_own.at[turn])
+        return pltpu.make_async_remote_copy(
+            source, target, back_send.at[turn, mask - 1], back_recv.at[turn, mask - 1],
+            device_id={"seq": other}, device_id_type=MESH)
+
+    def pass_copy(turn, mask):
+        columns = head_columns(turn, partner_of(me, mask))
+        return pltpu.make_async_remote_copy(
+            features.at[0, :, columns], features.at[1, :, columns], pass_send.at[turn, mask], pass_recv.at[turn, mask],
+            device_id={"win": before}, device_id_type=MESH)
+
+    def weight_copy(turn):
+        rows = pl.ds(turn * width, width)
+        return pltpu.make_async_copy(w_out.at[rows, :], weights.at[rows, :], weight_sem.at[turn])
+
+    blends[me] = jnp.broadcast_to(blend[...].astype(jnp.float32), (8, image_rows))
+    pl.semaphore_wait(barrier, len(masks) + 2)
+    for turn in range(min(2, rounds)):
+        send_keys(turn)
+        send_queries(turn)
+        if turn == 0:
+            for mask in masks:
+                blend_copy(mask).start()
+    for turn in range(rounds):
+        for copy in moves(turn, 0):
+            copy.start()
+    for turn in range(rounds):
+        weight_copy(turn).start()
+
+    if pad_rows:
+        zeros = jnp.zeros((rounds, pad_rows, HEAD_DIM), keys.dtype)
+        keys[:, all_image + count * text_rows :, :] = zeros
+        values[:, all_image + count * text_rows :, :] = zeros
+    given = jnp.where(prompt_ids[...] != 0, 0.0, -jnp.inf).astype(jnp.float32)
+    if pad_rows:
+        given = jnp.concatenate([given, jnp.full((1, pad_rows), -jnp.inf, jnp.float32)], axis=1)
+    scale = HEAD_DIM ** -0.5 * LOG2E
+    contract = (((1,), (1,)), ((), ()))
+
+    def attend(turn, mask):
+        place = partner_of(me, mask)
+        held = queries[turn, pl.ds(pl.multiple_of(place * image_rows, image_rows), image_rows), :]
+        image_scores = lax.dot_general(held, keys[turn, :all_image, :], contract, preferred_element_type=jnp.float32)
+        text_scores = lax.dot_general(held, keys[turn, all_image:, :], contract, preferred_element_type=jnp.float32) + given
+        peak = jnp.maximum(jnp.max(image_scores, axis=1, keepdims=True), jnp.max(text_scores, axis=1, keepdims=True))
+        image_weights = jnp.exp2((image_scores - peak) * scale)
+        text_weights = jnp.exp2((text_scores - peak) * scale)
+        total = jnp.sum(image_weights, axis=1, keepdims=True) + jnp.sum(text_weights, axis=1, keepdims=True)
+        product = jnp.dot(image_weights.astype(jnp.bfloat16), values[turn, :all_image, :], preferred_element_type=jnp.float32)
+        product += jnp.dot(text_weights.astype(jnp.bfloat16), values[turn, all_image:, :], preferred_element_type=jnp.float32)
+        attended = (product * (1.0 / total)).astype(jnp.bfloat16).reshape(strip_rows, WCOLS, HEAD_DIM)
+        left[turn, strip_place(mask), :] = attended[:, :STRIDE].reshape(strip_size, HEAD_DIM)
+        right[turn, strip_place(mask), :] = attended[:, STRIDE:].reshape(strip_size, HEAD_DIM)
+
+    def own_weight(mask):
+        token = lax.broadcasted_iota(jnp.int32, (strip_size, image_rows), 1)
+        spot = lax.broadcasted_iota(jnp.int32, (strip_size, image_rows), 0)
+        chosen = token == (spot // STRIDE) * WCOLS + spot % STRIDE
+        spread = jnp.where(chosen, blends[partner_of(me, mask)][:1, :], 0.0).astype(jnp.bfloat16)
+        return jnp.dot(spread, jnp.ones((image_rows, HEAD_DIM), jnp.bfloat16), preferred_element_type=jnp.float32)
+
+    def mix(turn, mask):
+        if turn == 0 and mask != 0:
+            blend_copy(mask, True).wait_recv()
+        strip_copy(turn, mask).wait_recv()
+        own = own_weight(mask)
+        mine = left[turn, strip_place(mask), :].astype(jnp.float32)
+        theirs = prev_right[turn, strip_place(mask), :].astype(jnp.float32)
+        mixed[turn, strip_place(mask), :] = ((own * mine + (blend_total - own) * theirs) * (1.0 / blend_total)).astype(jnp.bfloat16)
+        back_copy(turn, mask).start()
+
+    def pass_on(turn, order):
+        for mask in order:
+            copy = back_copy(turn, mask, True)
+            if mask == 0:
+                copy.wait()
+            else:
+                copy.wait_recv()
+            pass_copy(turn, mask).start()
+
+    tile = 512
+
+    def project(turn, halves):
+        first, final = turn == 0, turn == rounds - 1
+        low, high = halves[0] * strip_size, (halves[-1] + 1) * strip_size
+        rows = features[halves[0] : halves[-1] + 1, :, turn * width : (turn + 1) * width].reshape(high - low, width)
+
+        def one_tile(index, carry):
+            columns = pl.ds(pl.multiple_of(index * tile, tile), tile)
+            result = jnp.dot(rows, weights[turn * width : (turn + 1) * width, columns], preferred_element_type=jnp.float32)
+            if not first:
+                result = result + partial[low:high, columns]
+            if not final:
+                partial[low:high, columns] = result
+            else:
+                result = result.astype(jnp.bfloat16).reshape(len(halves), strip_rows, STRIDE, tile)
+                for place, half in enumerate(halves):
+                    out[:, half, :, columns] = result[place]
+            return carry
+
+        lax.fori_loop(0, weights.shape[1] // tile, one_tile, 0)
+
+    blocks = masks + [0]
+    for turn in range(rounds):
+        final = turn == rounds - 1
+        if final:
+            pass_on(turn - 1, blocks)
+        for mask in blocks:
+            arrived(turn, mask, range(4))
+        lag = 2
+        for step in range(len(blocks) + lag):
+            if step < len(blocks):
+                arrived(turn, blocks[step], [4])
+                attend(turn, blocks[step])
+                strip_copy(turn, blocks[step]).start()
+            if step >= lag:
+                mix(turn, blocks[step - lag])
+        if 2 <= turn + 1 < rounds:
+            send_queries(turn + 1)
+        if turn + 2 < rounds:
+            send_keys(turn + 2)
+        if turn >= 1 and not final:
+            pass_on(turn - 1, blocks)
+            if turn == 1:
+                for other in range(rounds):
+                    weight_copy(other).wait()
+            for mask in blocks:
+                pass_copy(turn - 1, mask).wait_recv()
+            project(turn - 1, (0, 1))
+
+    final = rounds - 1
+    pass_on(final, [0])
+    for mask in blocks:
+        pass_copy(final - 1, mask).wait_recv()
+    project(final - 1, (0, 1))
+    pass_on(final, masks[::-1])
+    project(final, (0,))
+    for mask in blocks:
+        pass_copy(final, mask).wait_recv()
+    project(final, (1,))
+
+    for turn in range(rounds):
+        for mask in blocks:
+            strip_copy(turn, mask).wait_send()
+            pass_copy(turn, mask).wait_send()
+            if mask != 0:
+                back_copy(turn, mask).wait_send()
+                for copy in moves(turn, mask):
+                    copy.wait_send()
+    for mask in masks:
+        blend_copy(mask).wait_send()
+
+
+def on_device_by_heads(query, key_image, value_image, key_text, value_text, prompt_ids, blend, w_out):
+    count = lax.axis_size("seq")
+    image_rows, text_rows = query.shape[1], key_text.shape[1]
+    rounds = query.shape[2] // HEAD_DIM // count
+    all_image = count * image_rows
+    key_rows = all_image + -(-count * text_rows // 128) * 128
+    strip_rows = image_rows // WCOLS
+    window_strip = (rounds, count * strip_rows * STRIDE, HEAD_DIM)
+    anywhere = pl.BlockSpec(memory_space=pl.ANY)
+    vmem = pl.BlockSpec(memory_space=pltpu.VMEM)
+    dma = pltpu.SemaphoreType.DMA
+    out = pl.pallas_call(
+        functools.partial(window_kernel, count, rounds),
+        out_shape=jax.ShapeDtypeStruct((strip_rows, 2, STRIDE, w_out.shape[1]), jnp.bfloat16),
+        in_specs=[anywhere] * 5 + [vmem] * 2 + [anywhere],
+        out_specs=vmem,
+        scratch_shapes=[
+            pltpu.VMEM((rounds, all_image, HEAD_DIM), jnp.bfloat16),
+            pltpu.VMEM((rounds, key_rows, HEAD_DIM), jnp.bfloat16),
+            pltpu.VMEM((rounds, key_rows, HEAD_DIM), jnp.bfloat16),
+            pltpu.VMEM(window_strip, jnp.bfloat16),
+            pltpu.VMEM(window_strip, jnp.bfloat16),
+            pltpu.VMEM(window_strip, jnp.bfloat16),
+            pltpu.VMEM(window_strip, jnp.bfloat16),
+            pltpu.VMEM((count, 8, image_rows), jnp.float32),
+            pltpu.VMEM((2, strip_rows * STRIDE, query.shape[2]), jnp.bfloat16),
+            pltpu.VMEM(w_out.shape, jnp.bfloat16),
+            pltpu.VMEM((image_rows, w_out.shape[1]), jnp.float32),
+            dma((rounds, count - 1, 5)),
+            dma((rounds, count - 1, 5)),
+            dma((rounds, 5)),
+            dma((count - 1,)),
+            dma((count - 1,)),
+            dma((rounds, count)),
+            dma((rounds, count)),
+            dma((rounds, count - 1)),
+            dma((rounds, count - 1)),
+            dma((rounds,)),
+            dma((rounds, count)),
+            dma((rounds, count)),
+            dma((rounds,)),
+        ],
+        compiler_params=pltpu.CompilerParams(
+            collective_id=0, has_side_effects=True, vmem_limit_bytes=VMEM_GRANT
+        ),
+    )(query, key_image, key_text, value_image, value_text, prompt_ids, blend, w_out)
+    return out.reshape(1, image_rows, w_out.shape[1])
+
+
 def solution(mesh):
+    seq_count = mesh.shape["seq"]
+    by_heads = seq_count > 1 and seq_count & (seq_count - 1) == 0 and HEADS % seq_count == 0
     placed = (
         P(("pano", "win"), "seq", None),
         P(("pano", "win"), "seq", None),
@@ -161,7 +477,7 @@
         P(),
     )
     return jax.shard_map(
-        on_device,
+        on_device_by_heads if by_heads else on_device,
         mesh=mesh,
         in_specs=placed,
         out_specs=P(("pano", "win"), "seq", None),

time: 139 us -> 67.4 us (0.48); the launches traced: 137 us -> 67.2 us
  waiting for transfers between devices: 85.4 us -> 0 us
  Pallas kernels: 0 us -> 64.9 us
  local copies, waits for them, and re-layouts: 19.8 us -> 2.36 us
  matrix products: 16.8 us -> 0 us
  starting transfers between devices: 8.29 us -> 0 us
  other arithmetic: 5.97 us -> 0 us
    ppermute x6 -> x0, waiting for transfers between devices: 85.4 us -> none  [the longest x4 80.8 us: swapped(): return lax.ppermute(block, axis, route)]
    pallas_call x0 -> x1, Pallas kernels: none -> 64.9 us  [on_device_by_heads(): pl.pallas_call(functools.partial(window_kernel, count, rounds), out_shape...]
    dot_general x5 -> x0, matrix products: 16.8 us -> none  [the longest x3 10.3 us: project_rows(): jnp.dot(flat_rows, w_out, preferred_element_type=jnp.float32)]
    ppermute x6 -> x0, starting transfers between devices: 8.29 us -> none  [the longest x4 4.51 us: swapped(): return lax.ppermute(block, axis, route)]
    dynamic_slice x3 -> x0, local copies, waits for them, and re-layouts: 6.48 us -> none  [the longest x1 5.11 us: regroup(): kept_half = lax.dynamic_index_in_dim(paired, own_bit, 2, keepdims=False)]
    concatenate x7 -> x0, local copies, waits for them, and re-layouts: 6.01 us -> none  [the longest x6 5.93 us: on_device(): jnp.concatenate([query[0], key_image[0], key_text[0], value_image[0], val...]
    unnamed x22 -> x1, local copies, waits for them, and re-layouts: 4.71 us -> 2.36 us
    reduce_sum x1 -> x0, other arithmetic: 2.22 us -> none  [absorb(): denominator = denominator * rescale + jnp.sum(weights, axis=2)]
  transfers between devices with their start and end apart: 6 -> 0, of which waited for: 5 -> 0; matrix products, arithmetic and copies ran while one was open for 5% -> 0% of each run, Pallas kernels for 0% -> 0%
where the time goes in v2:
time: 67.4 us; the launch traced here: 67.2 us
  Pallas kernels  64.9 us (96%)
  local copies, waits for them, and re-layouts  2.36 us (4%)
    pallas_call x1, Pallas kernels, on_device_by_heads(): pl.pallas_call(functools.partial(window_kernel, count, rounds), out_shape...  64.9 us
    unnamed x1, local copies, waits for them, and re-layouts  2.36 us

profile of v2, /device:TPU:1, one launch (start us, length us, event | category | flops | bytes accessed | tf_op | source)
XLA Modules:
  0.0 67.2 jit_solution(11834735143160308089)
XLA Ops:
  0.0 64.9 %shard_map.82 = bf16[3,2,32,3072]{3,2,1,0:T(8,128)(2,1)} custom-call(bf16[1,192,1536]{2,1,0:T(8,128)(2,1)} %query.1, bf16[1,192,1536]{2,1,0:T(8,128)(2,1)} %key_image.1, bf16[1,16,1536]{2,1,0:T(8,128)(2,1)} %key_text.1, bf16[1,192,1536]{2,1,0:T(8,128)(2,1)} %value_image.1, bf16[1,16,1536]{2,1,0:T(8,128)(2,1)} %value_text.1, s32[1,64]{1,0:T(1,128)} %prompt_ids.1, ...), custom_call_target="tpu_custom_call" | custom-call | tf_op jit(solution)/shard_map/pallas_call | solution.py:428
  64.9 2.4 %copy.10 = bf16[1,192,3072]{2,1,0:T(8,128)(2,1)} copy(bf16[1,192,3072]{2,1,0:T(8,128)(2,1)} %bitcast.1) | data formatting | bytes 2359296

commit v3 on v2

--- a/solution.py
+++ b/solution.py
@@ -157,7 +157,7 @@
 LOG2E = 1.4426950408889634
 
 
-VMEM_GRANT = 60 * 1024 * 1024
+VMEM_GRANT = 28 * 1024 * 1024
 
 
 def partner_of(position, mask):
@@ -173,7 +173,7 @@
     count, rounds, query, key_image, key_text, value_image, value_text, prompt_ids, blend, w_out,
     out, queries, keys, values, left, right, prev_right, mixed, blends, features, weights, partial,
     send_sem, recv_sem, own_sem, blend_send, blend_recv, strip_send, strip_recv,
-    back_send, back_recv, back_own, pass_send, pass_recv, weight_sem,
+    back_send, back_recv, back_own, pass_send, pass_recv, weight_sem, ids_held, blend_held, small_sem,
 ):
     image_rows = query.shape[1]
     text_rows = key_text.shape[1]
@@ -189,6 +189,12 @@
     before = lax.rem(window + windows - 1, windows)
     masks = list(range(count - 1, 0, -1))
 
+    small = [
+        pltpu.make_async_copy(prompt_ids, ids_held, small_sem.at[0]),
+        pltpu.make_async_copy(blend, blend_held, small_sem.at[1]),
+    ]
+    for copy in small:
+        copy.start()
     barrier = pltpu.get_barrier_semaphore()
     for mask in masks:
         pl.semaphore_signal(barrier, inc=1, device_id={"seq": partner_of(me, mask)}, device_id_type=MESH)
@@ -276,7 +282,9 @@
         rows = pl.ds(turn * width, width)
         return pltpu.make_async_copy(w_out.at[rows, :], weights.at[rows, :], weight_sem.at[turn])
 
-    blends[me] = jnp.broadcast_to(blend[...].astype(jnp.float32), (8, image_rows))
+    for copy in small:
+        copy.wait()
+    blends[me] = jnp.broadcast_to(blend_held[...].astype(jnp.float32), (8, image_rows))
     pl.semaphore_wait(barrier, len(masks) + 2)
     for turn in range(min(2, rounds)):
         send_keys(turn)
@@ -294,7 +302,7 @@
         zeros = jnp.zeros((rounds, pad_rows, HEAD_DIM), keys.dtype)
         keys[:, all_image + count * text_rows :, :] = zeros
         values[:, all_image + count * text_rows :, :] = zeros
-    given = jnp.where(prompt_ids[...] != 0, 0.0, -jnp.inf).astype(jnp.float32)
+    given = jnp.where(ids_held[...] != 0, 0.0, -jnp.inf).astype(jnp.float32)
     if pad_rows:
         given = jnp.concatenate([given, jnp.full((1, pad_rows), -jnp.inf, jnp.float32)], axis=1)
     scale = HEAD_DIM ** -0.5 * LOG2E
@@ -366,8 +374,6 @@
     blocks = masks + [0]
     for turn in range(rounds):
         final = turn == rounds - 1
-        if final:
-            pass_on(turn - 1, blocks)
         for mask in blocks:
             arrived(turn, mask, range(4))
         lag = 2
@@ -378,10 +384,9 @@
                 strip_copy(turn, blocks[step]).start()
             if step >= lag:
                 mix(turn, blocks[step - lag])
-        if 2 <= turn + 1 < rounds:
-            send_queries(turn + 1)
         if turn + 2 < rounds:
             send_keys(turn + 2)
+            send_queries(turn + 2)
         if turn >= 1 and not final:
             pass_on(turn - 1, blocks)
             if turn == 1:
@@ -392,6 +397,7 @@
             project(turn - 1, (0, 1))
 
     final = rounds - 1
+    pass_on(final - 1, blocks)
     pass_on(final, [0])
     for mask in blocks:
         pass_copy(final - 1, mask).wait_recv()
@@ -422,13 +428,17 @@
     key_rows = all_image + -(-count * text_rows // 128) * 128
     strip_rows = image_rows // WCOLS
     window_strip = (rounds, count * strip_rows * STRIDE, HEAD_DIM)
-    anywhere = pl.BlockSpec(memory_space=pl.ANY)
+    anywhere = pl.BlockSpec(memory_space=pltpu.HBM)
     vmem = pl.BlockSpec(memory_space=pltpu.VMEM)
     dma = pltpu.SemaphoreType.DMA
+    operands = [
+        pltpu.with_memory_space_constraint(operand, pltpu.HBM)
+        for operand in (query, key_image, key_text, value_image, value_text, prompt_ids, blend, w_out)
+    ]
     out = pl.pallas_call(
         functools.partial(window_kernel, count, rounds),
         out_shape=jax.ShapeDtypeStruct((strip_rows, 2, STRIDE, w_out.shape[1]), jnp.bfloat16),
-        in_specs=[anywhere] * 5 + [vmem] * 2 + [anywhere],
+        in_specs=[anywhere] * 8,
         out_specs=vmem,
         scratch_shapes=[
             pltpu.VMEM((rounds, all_image, HEAD_DIM), jnp.bfloat16),
@@ -455,11 +465,14 @@
             dma((rounds, count)),
             dma((rounds, count)),
             dma((rounds,)),
+            pltpu.VMEM(prompt_ids.shape, prompt_ids.dtype),
+            pltpu.VMEM(blend.shape, blend.dtype),
+            dma((2,)),
         ],
         compiler_params=pltpu.CompilerParams(
             collective_id=0, has_side_effects=True, vmem_limit_bytes=VMEM_GRANT
         ),
-    )(query, key_image, key_text, value_image, value_text, prompt_ids, blend, w_out)
+    )(*operands)
     return out.reshape(1, image_rows, w_out.shape[1])
 
 

time: 67.4 us -> 64.3 us (0.954)
  Pallas kernels: 64.9 us -> 63.1 us
  local copies, waits for them, and re-layouts: 2.36 us -> 1.02 us
    pallas_call x1, Pallas kernels: 64.9 us -> 63.1 us  [on_device_by_heads(): pl.pallas_call(functools.partial(window_kernel, count, rounds), out_shape...]
    unnamed x1, local copies, waits for them, and re-layouts: 2.36 us -> 1.02 us
where the time goes in v3:
time: 64.3 us; the launch traced here: 64.1 us
  Pallas kernels  63.1 us (98%)
  local copies, waits for them, and re-layouts  1.02 us (2%)
    pallas_call x1, Pallas kernels, on_device_by_heads(): pl.pallas_call(functools.partial(window_kernel, count, rounds), out_shape...  63.1 us

profile of v3, /device:TPU:1, one launch (start us, length us, event | category | flops | bytes accessed | tf_op | source)
XLA Modules:
  0.0 64.1 jit_solution(1738481508534995187)
XLA Ops:
  0.0 63.1 %shard_map.82 = bf16[3,2,32,3072]{3,2,1,0:T(8,128)(2,1)S(1)} custom-call(bf16[1,192,1536]{2,1,0:T(8,128)(2,1)} %query.1, bf16[1,192,1536]{2,1,0:T(8,128)(2,1)} %key_image.1, bf16[1,16,1536]{2,1,0:T(8,128)(2,1)} %key_text.1, bf16[1,192,1536]{2,1,0:T(8,128)(2,1)} %value_image.1, bf16[1,16,1536]{2,1,0:T(8,128)(2,1)} %value_text.1, s32[1,64]{1,0:T(1,128)} %prompt_ids.1, ...), custom_call_target="tpu_custom_call" | custom-call | tf_op jit(solution)/shard_map/pallas_call | solution.py:438
  63.1 1.0 %copy.10 = bf16[1,192,3072]{2,1,0:T(8,128)(2,1)} copy(bf16[1,192,3072]{2,1,0:T(8,128)(2,1)S(1)} %bitcast.1) | data formatting | bytes 2359296

commit v4 on v3

--- a/solution.py
+++ b/solution.py
@@ -376,12 +376,14 @@
         final = turn == rounds - 1
         for mask in blocks:
             arrived(turn, mask, range(4))
-        lag = 2
+        lag = min(3, count)
         for step in range(len(blocks) + lag):
             if step < len(blocks):
                 arrived(turn, blocks[step], [4])
                 attend(turn, blocks[step])
                 strip_copy(turn, blocks[step]).start()
+            if step == len(blocks) and final:
+                pass_on(turn - 1, blocks)
             if step >= lag:
                 mix(turn, blocks[step - lag])
         if turn + 2 < rounds:
@@ -397,7 +399,6 @@
             project(turn - 1, (0, 1))
 
     final = rounds - 1
-    pass_on(final - 1, blocks)
     pass_on(final, [0])
     for mask in blocks:
         pass_copy(final - 1, mask).wait_recv()

time: 64.3 us -> 64.2 us (level)
  no operation moved by 1% of the time
where the time goes in v4:
time: 64.2 us; the launch traced here: 64 us
  Pallas kernels  63 us (98%)
  local copies, waits for them, and re-layouts  1.02 us (2%)
    pallas_call x1, Pallas kernels, on_device_by_heads(): pl.pallas_call(functools.partial(window_kernel, count, rounds), out_shape...  63 us

profile of v4, /device:TPU:1, one launch (start us, length us, event | category | flops | bytes accessed | tf_op | source)
XLA Modules:
  0.0 64.0 jit_solution(2839329724600981247)
XLA Ops:
  0.0 63.0 %shard_map.82 = bf16[3,2,32,3072]{3,2,1,0:T(8,128)(2,1)S(1)} custom-call(bf16[1,192,1536]{2,1,0:T(8,128)(2,1)} %query.1, bf16[1,192,1536]{2,1,0:T(8,128)(2,1)} %key_image.1, bf16[1,16,1536]{2,1,0:T(8,128)(2,1)} %key_text.1, bf16[1,192,1536]{2,1,0:T(8,128)(2,1)} %value_image.1, bf16[1,16,1536]{2,1,0:T(8,128)(2,1)} %value_text.1, s32[1,64]{1,0:T(1,128)} %prompt_ids.1, ...), custom_call_target="tpu_custom_call" | custom-call | tf_op jit(solution)/shard_map/pallas_call | solution.py:439
  63.0 1.0 %copy.10 = bf16[1,192,3072]{2,1,0:T(8,128)(2,1)} copy(bf16[1,192,3072]{2,1,0:T(8,128)(2,1)S(1)} %bitcast.1) | data formatting | bytes 2359296
